TPU v7x, 512 devices: a whole 4x8x8 slice. The times are simulated.
512 devices in a mesh: band: 32 (over z_lo, y, core), dom: 16 (over z_hi, x).
Axes of the slice: x: 4, y: 8, z: 8 (z_hi: 4, z_lo: 2; z = z_hi * 2 + z_lo), core: 2. Of those that a mesh axis runs over, the one named last changes fastest.
Arguments:
- states: float32 [4096, 8, 128, 128], P('band', None, 'dom'), may hold values from -0.015625 to 0.015625
- window: float32 [128, 8, 128, 128], P('band', None, 'dom'), may hold values from -6 to 6
- potential: float32 [8, 128, 128], P(None, 'dom'), may hold values from -3 to 3
Outputs:
- intersection: float32 [4096, 128], P('band')
- hamiltonian: float32 [4096, 128], P('band')
All inputs are finite; a program needn't handle non-finite values.
Results may differ from a plain program's by a relative error of at most 0.00012.
Values sent between devices are 32-bit elements; how exact they have to be, the bound alone decides.
A program may use at most 64 MiB of HBM per device.

v0:
```python
import jax
import jax.numpy as jnp
from jax import lax
from jax.sharding import PartitionSpec as P

DEGREE = 4
coeffs = (
    -5369.0 / 1800.0,
    12.0 / 7.0,
    -15.0 / 56.0,
    10.0 / 189.0,
    -1.0 / 112.0,
    2.0 / 1925.0,
    -1.0 / 16632.0,
)
centre_value = 9.0
half_width = 7.0


def padded(block, sides, width):
    for axis, dim in sides:
        count = lax.axis_size(axis)
        forward = [(i, i + 1) for i in range(count - 1)]
        forward.append((count - 1, 0))
        backward = [(target, source) for source, target in forward]
        low = lax.ppermute(
            lax.slice_in_dim(block, block.shape[dim] - width, None, axis=dim), axis, forward
        )
        high = lax.ppermute(lax.slice_in_dim(block, 0, width, axis=dim), axis, backward)
        block = jnp.concatenate([low, block, high], axis=dim)
    return block


def stencil_sum(wave_in, padded_x, padded_y, potential):
    x_cells = wave_in.shape[2]
    y_cells = wave_in.shape[3]
    z_cells = wave_in.shape[1]
    along_z = jnp.pad(wave_in, ((0, 0), (6, 6), (0, 0), (0, 0)))
    laplace = 3.0 * coeffs[0] * wave_in
    for offset in range(1, 7):
        beside = (
            padded_x[:, :, 6 + offset : 6 + offset + x_cells]
            + padded_x[:, :, 6 - offset : 6 - offset + x_cells]
        )
        beside = (
            beside
            + padded_y[:, :, :, 6 + offset : 6 + offset + y_cells]
            + padded_y[:, :, :, 6 - offset : 6 - offset + y_cells]
        )
        beside = (
            beside
            + along_z[:, 6 + offset : 6 + offset + z_cells]
            + along_z[:, 6 - offset : 6 - offset + z_cells]
        )
        laplace = laplace + coeffs[offset] * beside
    return -0.5 * laplace + potential * wave_in


def apply_banded(wave_in, potential):
    padded_x = padded(wave_in, (("dom", 2),), 6)
    padded_y = jnp.concatenate((wave_in[:, :, :, -6:], wave_in, wave_in[:, :, :, :6]), axis=3)
    return stencil_sum(wave_in, padded_x, padded_y, potential)


def chebyshev(window, operate):
    previous = window
    current = (operate(window) - centre_value * window) / half_width
    for repeat_index in range(DEGREE - 1):
        following = 2.0 * (operate(current) - centre_value * current) / half_width - previous
        previous, current = (current, following)
    image = operate(current)
    return jnp.stack((current, image))


def per_device(states, window, potential):
    stacked = chebyshev(window, lambda wave: apply_banded(wave, potential))
    states_flat = states.reshape(states.shape[0], -1)
    whole_window = lax.all_gather(stacked, "band", axis=1, tiled=True)
    flat_piece = whole_window.reshape(-1, states_flat.shape[1])
    product = lax.dot_general(
        states_flat,
        flat_piece,
        (((1,), (1,)), ((), ())),
        precision=lax.Precision.HIGHEST,
        preferred_element_type=jnp.float32,
    )
    partial_value = product.reshape(states_flat.shape[0], 2, whole_window.shape[1])
    totals = lax.psum(partial_value, "dom")
    return (totals[:, 0, :], totals[:, 1, :])


def solution(mesh):
    in_specs = (P("band", None, "dom", None), P("band", None, "dom", None), P(None, "dom", None))
    out_specs = (P("band", None), P("band", None))
    return jax.shard_map(
        per_device, mesh=mesh, in_specs=in_specs, out_specs=out_specs, check_vma=False
    )
```

profile of v0, /device:TPU:8, one launch (start us, length us, event | category | flops | bytes accessed | tf_op | source)
XLA Modules:
  0.0 371.7 jit_solution(3588212571015930287)
XLA Ops:
  7.2 1.0 fusion.338
  8.2 13.1 %collective-permute-start = (f32[4,8,6,128]{3,2,1,0:T(8,128)S(1)}, f32[4,8,6,128]{3,2,1,0:T(8,128)S(1)}, u32[]{:S(2)}, u32[]{:S(2)}) collective-permute-start(f32[4,8,6,128]{3,2,1,0:T(8,128)S(1)} %get-tuple-element.22), channel_id=1, source_target_pairs={{1,0},{2,1},{3,2},{4,3},{5,4},{6,5},{7,6},{8,7},{9,8},{10,9},{11,1... | collective-permute-start | bytes 294920 | tf_op jit(solution)/shard_map/ppermute | solution.py:29
  21.4 1.9 collective-permute-start.1
  23.3 1.1 fusion.339
  25.1 0.9 constant_dynamic-update-slice_fusion.1
  26.9 7.5 %collective-permute-done.1 = f32[4,8,6,128]{3,2,1,0:T(8,128)S(1)} collective-permute-done((f32[4,8,6,128]{3,2,1,0:T(8,128)S(1)}, f32[4,8,6,128]{3,2,1,0:T(8,128)S(1)}, u32[]{:S(2)}, u32[]{:S(2)}) %collective-permute-start.1) | collective-permute-done | bytes 98336 | tf_op jit(solution)/shard_map/ppermute | solution.py:26
  34.5 5.2 %broadcast_multiply_fusion = (f32[4,8,8,128]{3,2,1,0:T(8,128)S(1)}, f32[4,8,8,128]{3,2,1,0:T(8,128)S(1)}) fusion(f32[4,8,8,128]{3,2,1,0:T(8,128)} %param.4, f32[8,8,128]{2,1,0:T(8,128)} %param.5, f32[4,8,8,6]{3,2,1,0:T(8,128)S(1)} %get-tuple-element.25, f32[4,8,8,6]{3,2,1,0:T(8,128)S(1)} %get-tuple-element.24, ...), kind=kLoop, calls=%fused_computation.601 | loop fusion | flops 2195456 | bytes 1323008 | tf_op jit(solution)/shard_map/div | solution.py:67
  39.7 1.9 collective-permute-start.2
  41.6 3.9 %collective-permute-start.3 = (f32[4,8,6,128]{3,2,1,0:T(8,128)S(1)}, f32[4,8,6,128]{3,2,1,0:T(8,128)S(1)}, u32[]{:S(2)}, u32[]{:S(2)}) collective-permute-start(f32[4,8,6,128]{3,2,1,0:T(8,128)S(1)} %get-tuple-element.19), channel_id=1, source_target_pairs={{0,1},{1,2},{2,3},{3,4},{4,5},{5,6},{6,7},{7,8},{8,9},{9,10},{10,1... | collective-permute-start | bytes 294920 | tf_op jit(solution)/shard_map/ppermute | solution.py:26
  45.7 1.8 collective-permute-done.2
  47.5 7.0 %collective-permute-done.3 = f32[4,8,6,128]{3,2,1,0:T(8,128)S(1)} collective-permute-done((f32[4,8,6,128]{3,2,1,0:T(8,128)S(1)}, f32[4,8,6,128]{3,2,1,0:T(8,128)S(1)}, u32[]{:S(2)}, u32[]{:S(2)}) %collective-permute-start.3) | collective-permute-done | bytes 98336 | tf_op jit(solution)/shard_map/ppermute | solution.py:26
  54.5 1.8 fusion.195
  56.2 1.9 collective-permute-start.4
  58.2 3.9 %collective-permute-start.5 = (f32[4,8,6,128]{3,2,1,0:T(8,128)S(1)}, f32[4,8,6,128]{3,2,1,0:T(8,128)S(1)}, u32[]{:S(2)}, u32[]{:S(2)}) collective-permute-start(f32[4,8,6,128]{3,2,1,0:T(8,128)S(1)} %get-tuple-element.15), channel_id=1, source_target_pairs={{0,1},{1,2},{2,3},{3,4},{4,5},{5,6},{6,7},{7,8},{8,9},{9,10},{10,1... | collective-permute-start | bytes 294920 | tf_op jit(solution)/shard_map/ppermute | solution.py:26
  62.2 0.9 collective-permute-done.4
  63.1 6.2 %collective-permute-done.5 = f32[4,8,6,128]{3,2,1,0:T(8,128)S(1)} collective-permute-done((f32[4,8,6,128]{3,2,1,0:T(8,128)S(1)}, f32[4,8,6,128]{3,2,1,0:T(8,128)S(1)}, u32[]{:S(2)}, u32[]{:S(2)}) %collective-permute-start.5) | collective-permute-done | bytes 98336 | tf_op jit(solution)/shard_map/ppermute | solution.py:26
  69.3 1.6 fusion.134
  70.9 1.9 collective-permute-start.6
  72.9 3.9 %collective-permute-start.7 = (f32[4,8,6,128]{3,2,1,0:T(8,128)S(1)}, f32[4,8,6,128]{3,2,1,0:T(8,128)S(1)}, u32[]{:S(2)}, u32[]{:S(2)}) collective-permute-start(f32[4,8,6,128]{3,2,1,0:T(8,128)S(1)} %get-tuple-element.11), channel_id=1, source_target_pairs={{0,1},{1,2},{2,3},{3,4},{4,5},{5,6},{6,7},{7,8},{8,9},{9,10},{10,1... | collective-permute-start | bytes 294920 | tf_op jit(solution)/shard_map/ppermute | solution.py:26
  76.9 0.9 collective-permute-done.6
  77.8 6.8 %collective-permute-done.7 = f32[4,8,6,128]{3,2,1,0:T(8,128)S(1)} collective-permute-done((f32[4,8,6,128]{3,2,1,0:T(8,128)S(1)}, f32[4,8,6,128]{3,2,1,0:T(8,128)S(1)}, u32[]{:S(2)}, u32[]{:S(2)}) %collective-permute-start.7) | collective-permute-done | bytes 98336 | tf_op jit(solution)/shard_map/ppermute | solution.py:26
  84.6 0.9 fusion.73
  85.5 1.9 collective-permute-start.8
  87.4 3.9 %collective-permute-start.9 = (f32[4,8,6,128]{3,2,1,0:T(8,128)S(1)}, f32[4,8,6,128]{3,2,1,0:T(8,128)S(1)}, u32[]{:S(2)}, u32[]{:S(2)}) collective-permute-start(f32[4,8,6,128]{3,2,1,0:T(8,128)S(1)} %get-tuple-element.7), channel_id=1, source_target_pairs={{0,1},{1,2},{2,3},{3,4},{4,5},{5,6},{6,7},{7,8},{8,9},{9,10},{10,1... | collective-permute-start | bytes 294920 | tf_op jit(solution)/shard_map/ppermute | solution.py:26
  91.4 0.9 collective-permute-done.8
  92.3 6.1 %collective-permute-done.9 = f32[4,8,6,128]{3,2,1,0:T(8,128)S(1)} collective-permute-done((f32[4,8,6,128]{3,2,1,0:T(8,128)S(1)}, f32[4,8,6,128]{3,2,1,0:T(8,128)S(1)}, u32[]{:S(2)}, u32[]{:S(2)}) %collective-permute-start.9) | collective-permute-done | bytes 98336 | tf_op jit(solution)/shard_map/ppermute | solution.py:26
  98.5 0.9 fusion.12
  100.1 69.7 %all-gather.2.cloned.1.call-done = f32[2,128,8,8,128]{4,3,2,1,0:T(8,128)} async-done(((f32[2,4,8,8,128]{4,3,2,1,0:T(8,128)}), f32[2,128,8,8,128]{4,3,2,1,0:T(8,128)}) %all-gather.2.cloned.1.call-update) | async-done | bytes 8388624 | tf_op jit(solution)/shard_map/all_gather | solution.py:78
  169.9 9.4 %reshape.14 = f32[256,8192]{1,0:T(8,128)} reshape(f32[2,128,8,8,128]{4,3,2,1,0:T(8,128)} %all-gather.2.cloned.1.call-done) | data formatting | bytes 16777216 | tf_op jit(solution)/shard_map/reshape | solution.py:79
  179.2 11.7 %fusion = f32[256,128]{1,0:T(8,128)S(1)} fusion(f32[256,8192]{1,0:T(8,128)} %reshape.14, f32[16,8,64,128]{3,2,1,0:T(8,128)} %bitcast.19), kind=kOutput, calls=%fused_computation | convolution fusion | flops 3221225472 | bytes 12713984 | tf_op jit(solution)/shard_map/dot_general | solution.py:80
  191.7 171.6 %all-reduce.7.cloned.1.call-done = f32[128,2,128]{2,0,1:T(8,128)} async-done(((f32[128,2,128]{2,0,1:T(8,128)}), f32[128,2,128]{2,0,1:T(8,128)}) %all-reduce.7.cloned.1.call-update) | async-done | bytes 131088 | tf_op jit(solution)/shard_map/psum | solution.py:88
  363.4 1.5 slice_bitcast_fusion
  (19 shorter events, 3.7 us)
Async XLA Ops:
  7.2 77.4 %copy-start = (f32[8,8,128]{2,1,0:T(8,128)S(1)}, f32[8,8,128]{2,1,0:T(8,128)}, u32[]{:S(2)}) copy-start(f32[8,8,128]{2,1,0:T(8,128)} %param.5) | copy-start | bytes 98308
  7.2 162.7 %all-gather.2.cloned.1.call-start = ((), (), s32[]{:S(2)}) async-start(), calls=%async_computation | async-start | bytes 8650752 | tf_op jit(solution)/shard_map/all_gather | solution.py:78
  8.2 18.7 %collective-permute-start = (f32[4,8,6,128]{3,2,1,0:T(8,128)S(1)}, f32[4,8,6,128]{3,2,1,0:T(8,128)S(1)}, u32[]{:S(2)}, u32[]{:S(2)}) collective-permute-start(f32[4,8,6,128]{3,2,1,0:T(8,128)S(1)} %get-tuple-element.22), channel_id=1, source_target_pairs={{1,0},{2,1},{3,2},{4,3},{5,4},{6,5},{7,6},{8,7},{9,8},{10,9},{11,1... | collective-permute-start | bytes 294920 | tf_op jit(solution)/shard_map/ppermute | solution.py:29
  21.4 13.1 %collective-permute-start.1 = (f32[4,8,6,128]{3,2,1,0:T(8,128)S(1)}, f32[4,8,6,128]{3,2,1,0:T(8,128)S(1)}, u32[]{:S(2)}, u32[]{:S(2)}) collective-permute-start(f32[4,8,6,128]{3,2,1,0:T(8,128)S(1)} %get-tuple-element.23), channel_id=1, source_target_pairs={{0,1},{1,2},{2,3},{3,4},{4,5},{5,6},{6,7},{7,8},{8,9},{9,10},{10,1... | collective-permute-start | bytes 294920 | tf_op jit(solution)/shard_map/ppermute | solution.py:26
  39.7 7.8 %collective-permute-start.2 = (f32[4,8,6,128]{3,2,1,0:T(8,128)S(1)}, f32[4,8,6,128]{3,2,1,0:T(8,128)S(1)}, u32[]{:S(2)}, u32[]{:S(2)}) collective-permute-start(f32[4,8,6,128]{3,2,1,0:T(8,128)S(1)} %get-tuple-element.18), channel_id=1, source_target_pairs={{1,0},{2,1},{3,2},{4,3},{5,4},{6,5},{7,6},{8,7},{9,8},{10,9},{11,1... | collective-permute-start | bytes 294920 | tf_op jit(solution)/shard_map/ppermute | solution.py:29
  41.6 12.8 %collective-permute-start.3 = (f32[4,8,6,128]{3,2,1,0:T(8,128)S(1)}, f32[4,8,6,128]{3,2,1,0:T(8,128)S(1)}, u32[]{:S(2)}, u32[]{:S(2)}) collective-permute-start(f32[4,8,6,128]{3,2,1,0:T(8,128)S(1)} %get-tuple-element.19), channel_id=1, source_target_pairs={{0,1},{1,2},{2,3},{3,4},{4,5},{5,6},{6,7},{7,8},{8,9},{9,10},{10,1... | collective-permute-start | bytes 294920 | tf_op jit(solution)/shard_map/ppermute | solution.py:26
  56.2 6.9 %collective-permute-start.4 = (f32[4,8,6,128]{3,2,1,0:T(8,128)S(1)}, f32[4,8,6,128]{3,2,1,0:T(8,128)S(1)}, u32[]{:S(2)}, u32[]{:S(2)}) collective-permute-start(f32[4,8,6,128]{3,2,1,0:T(8,128)S(1)} %get-tuple-element.14), channel_id=1, source_target_pairs={{1,0},{2,1},{3,2},{4,3},{5,4},{6,5},{7,6},{8,7},{9,8},{10,9},{11,1... | collective-permute-start | bytes 294920 | tf_op jit(solution)/shard_map/ppermute | solution.py:29
  58.2 11.1 %collective-permute-start.5 = (f32[4,8,6,128]{3,2,1,0:T(8,128)S(1)}, f32[4,8,6,128]{3,2,1,0:T(8,128)S(1)}, u32[]{:S(2)}, u32[]{:S(2)}) collective-permute-start(f32[4,8,6,128]{3,2,1,0:T(8,128)S(1)} %get-tuple-element.15), channel_id=1, source_target_pairs={{0,1},{1,2},{2,3},{3,4},{4,5},{5,6},{6,7},{7,8},{8,9},{9,10},{10,1... | collective-permute-start | bytes 294920 | tf_op jit(solution)/shard_map/ppermute | solution.py:26
  70.9 6.9 %collective-permute-start.6 = (f32[4,8,6,128]{3,2,1,0:T(8,128)S(1)}, f32[4,8,6,128]{3,2,1,0:T(8,128)S(1)}, u32[]{:S(2)}, u32[]{:S(2)}) collective-permute-start(f32[4,8,6,128]{3,2,1,0:T(8,128)S(1)} %get-tuple-element.10), channel_id=1, source_target_pairs={{1,0},{2,1},{3,2},{4,3},{5,4},{6,5},{7,6},{8,7},{9,8},{10,9},{11,1... | collective-permute-start | bytes 294920 | tf_op jit(solution)/shard_map/ppermute | solution.py:29
  72.9 11.7 %collective-permute-start.7 = (f32[4,8,6,128]{3,2,1,0:T(8,128)S(1)}, f32[4,8,6,128]{3,2,1,0:T(8,128)S(1)}, u32[]{:S(2)}, u32[]{:S(2)}) collective-permute-start(f32[4,8,6,128]{3,2,1,0:T(8,128)S(1)} %get-tuple-element.11), channel_id=1, source_target_pairs={{0,1},{1,2},{2,3},{3,4},{4,5},{5,6},{6,7},{7,8},{8,9},{9,10},{10,1... | collective-permute-start | bytes 294920 | tf_op jit(solution)/shard_map/ppermute | solution.py:26
  85.5 6.9 %collective-permute-start.8 = (f32[4,8,6,128]{3,2,1,0:T(8,128)S(1)}, f32[4,8,6,128]{3,2,1,0:T(8,128)S(1)}, u32[]{:S(2)}, u32[]{:S(2)}) collective-permute-start(f32[4,8,6,128]{3,2,1,0:T(8,128)S(1)} %get-tuple-element.6), channel_id=1, source_target_pairs={{1,0},{2,1},{3,2},{4,3},{5,4},{6,5},{7,6},{8,7},{9,8},{10,9},{11,1... | collective-permute-start | bytes 294920 | tf_op jit(solution)/shard_map/ppermute | solution.py:29
  87.4 11.1 %collective-permute-start.9 = (f32[4,8,6,128]{3,2,1,0:T(8,128)S(1)}, f32[4,8,6,128]{3,2,1,0:T(8,128)S(1)}, u32[]{:S(2)}, u32[]{:S(2)}) collective-permute-start(f32[4,8,6,128]{3,2,1,0:T(8,128)S(1)} %get-tuple-element.7), channel_id=1, source_target_pairs={{0,1},{1,2},{2,3},{3,4},{4,5},{5,6},{6,7},{7,8},{8,9},{9,10},{10,1... | collective-permute-start | bytes 294920 | tf_op jit(solution)/shard_map/ppermute | solution.py:26
  100.1 263.3 %all-reduce.7.cloned.1.call-start = ((), (), s32[]{:S(2)}) async-start(), calls=%async_computation.1 | async-start | bytes 262144 | tf_op jit(solution)/shard_map/psum | solution.py:88
Sparse Core Ops, SparseCore 0:
  100.2 69.6 all-gather.1
  191.9 171.4 all-reduce.6
where the time goes:
time: 373 us; the launch traced here: 372 us
  waiting for transfers between devices  280 us (75%)
  starting transfers between devices  38.5 us (10%)
  local copies, waits for them, and re-layouts  15.1 us (4%)
  between operations  14.2 us (4%)
  other arithmetic  11.8 us (3%)
  matrix products  11.7 us (3%)
    psum x1, waiting for transfers between devices, per_device(): totals = lax.psum(partial_value, 'dom')  172 us
    all_gather x1, waiting for transfers between devices, per_device(): whole_window = lax.all_gather(stacked, 'band', axis=1, tiled=True)  69.7 us
    ppermute x5, waiting for transfers between devices, padded(): lax.ppermute(lax.slice_in_dim(block, block.shape[dim] - width, None, axis...  33.6 us
    ppermute x5, starting transfers between devices, padded(): lax.ppermute(lax.slice_in_dim(block, 0, width, axis=dim), axis, backward)  20.8 us
    ppermute x5, starting transfers between devices, padded(): lax.ppermute(lax.slice_in_dim(block, block.shape[dim] - width, None, axis...  17.6 us
    dot_general x1, matrix products, per_device(): lax.dot_general(states_flat, flat_piece, (((1,), (1,)), ((), ())), precis...  11.7 us
    reshape x1, local copies, waits for them, and re-layouts, per_device(): flat_piece = whole_window.reshape(-1, states_flat.shape[1])  9.36 us
  transfers between devices with their start and end apart: 12, of which 12 were waited for; matrix products, arithmetic and copies ran while one was open for 1% of the time, Pallas kernels for 0%

commit v1 on v0

--- a/solution.py
+++ b/solution.py
@@ -75,7 +75,9 @@
 def per_device(states, window, potential):
     stacked = chebyshev(window, lambda wave: apply_banded(wave, potential))
     states_flat = states.reshape(states.shape[0], -1)
-    whole_window = lax.all_gather(stacked, "band", axis=1, tiled=True)
+    whole_window = jnp.concatenate(
+        lax.all_to_all(jnp.stack([stacked] * lax.axis_size("band")), "band", 0, 0), axis=1
+    )
     flat_piece = whole_window.reshape(-1, states_flat.shape[1])
     product = lax.dot_general(
         states_flat,

time: 373 us -> 493 us (1.32)
  blocking collectives: 0 us -> 196 us
  waiting for transfers between devices: 280 us -> 200 us
  local copies, waits for them, and re-layouts: 15.1 us -> 20.2 us
    all_to_all x0 -> x1, blocking collectives: none -> 196 us  [per_device(): lax.all_to_all(jnp.stack([stacked] * lax.axis_size('band')), 'band', 0, 0)]
    all_gather x1 -> x0, waiting for transfers between devices: 69.7 us -> none  [per_device(): whole_window = lax.all_gather(stacked, 'band', axis=1, tiled=True)]
    another operation x0 -> x2, local copies, waits for them, and re-layouts: none -> 10.4 us  [the longest x1 9.37 us: per_device(): flat_piece = whole_window.reshape(-1, states_flat.shape[1])]
    psum x1, waiting for transfers between devices: 172 us -> 161 us  [per_device(): totals = lax.psum(partial_value, 'dom')]
    reshape x1, local copies, waits for them, and re-layouts: 9.36 us -> 4.1 us  [per_device(): jnp.concatenate(lax.all_to_all(jnp.stack([stacked] * lax.axis_size('band'...]
  transfers between devices with their start and end apart: 12 -> 11, of which waited for: 12 -> 11; matrix products, arithmetic and copies ran while one was open for 1% -> 1% of each run, Pallas kernels for 0% -> 0%
where the time goes in v1:
time: 493 us; the launch traced here: 492 us
  waiting for transfers between devices  200 us (41%)
  blocking collectives  196 us (40%)
  starting transfers between devices  38.5 us (8%)
  local copies, waits for them, and re-layouts  20.2 us (4%)
  between operations  14.2 us (3%)
  matrix products  11.7 us (2%)
  other arithmetic  11.1 us (2%)
    all_to_all x1, blocking collectives, per_device(): lax.all_to_all(jnp.stack([stacked] * lax.axis_size('band')), 'band', 0, 0)  196 us
    psum x1, waiting for transfers between devices, per_device(): totals = lax.psum(partial_value, 'dom')  161 us
    ppermute x5, waiting for transfers between devices, padded(): lax.ppermute(lax.slice_in_dim(block, block.shape[dim] - width, None, axis...  33.6 us
    ppermute x5, starting transfers between devices, padded(): lax.ppermute(lax.slice_in_dim(block, 0, width, axis=dim), axis, backward)  20.8 us
    ppermute x5, starting transfers between devices, padded(): lax.ppermute(lax.slice_in_dim(block, block.shape[dim] - width, None, axis...  17.6 us
    dot_general x1, matrix products, per_device(): lax.dot_general(states_flat, flat_piece, (((1,), (1,)), ((), ())), precis...  11.7 us
  transfers between devices with their start and end apart: 11, of which 11 were waited for; matrix products, arithmetic and copies ran while one was open for 1% of the time, Pallas kernels for 0%

profile of v1, /device:TPU:8, one launch (start us, length us, event | category | flops | bytes accessed | tf_op | source)
XLA Modules:
  0.0 492.2 jit_solution(3551801408100975676)
XLA Ops:
  7.2 1.0 fusion.338
  8.2 13.1 %collective-permute-start = (f32[4,8,6,128]{3,2,1,0:T(8,128)S(1)}, f32[4,8,6,128]{3,2,1,0:T(8,128)S(1)}, u32[]{:S(2)}, u32[]{:S(2)}) collective-permute-start(f32[4,8,6,128]{3,2,1,0:T(8,128)S(1)} %get-tuple-element.22), channel_id=1, source_target_pairs={{1,0},{2,1},{3,2},{4,3},{5,4},{6,5},{7,6},{8,7},{9,8},{10,9},{11,1... | collective-permute-start | bytes 294920 | tf_op jit(solution)/shard_map/ppermute | solution.py:29
  21.4 1.9 collective-permute-start.1
  23.3 1.1 fusion.339
  25.1 0.9 constant_dynamic-update-slice_fusion.1
  26.9 7.5 %collective-permute-done.1 = f32[4,8,6,128]{3,2,1,0:T(8,128)S(1)} collective-permute-done((f32[4,8,6,128]{3,2,1,0:T(8,128)S(1)}, f32[4,8,6,128]{3,2,1,0:T(8,128)S(1)}, u32[]{:S(2)}, u32[]{:S(2)}) %collective-permute-start.1) | collective-permute-done | bytes 98336 | tf_op jit(solution)/shard_map/ppermute | solution.py:26
  34.5 5.2 %broadcast_multiply_fusion = (f32[4,8,8,128]{3,2,1,0:T(8,128)S(1)}, f32[4,8,8,128]{3,2,1,0:T(8,128)S(1)}) fusion(f32[4,8,8,128]{3,2,1,0:T(8,128)} %param.4, f32[8,8,128]{2,1,0:T(8,128)} %param.5, f32[4,8,8,6]{3,2,1,0:T(8,128)S(1)} %get-tuple-element.25, f32[4,8,8,6]{3,2,1,0:T(8,128)S(1)} %get-tuple-element.24, ...), kind=kLoop, calls=%fused_computation.601 | loop fusion | flops 2195456 | bytes 1323008 | tf_op jit(solution)/shard_map/div | solution.py:67
  39.7 1.9 collective-permute-start.2
  41.6 3.9 collective-permute-start.3
  45.7 1.8 collective-permute-done.2
  47.5 7.0 %collective-permute-done.3 = f32[4,8,6,128]{3,2,1,0:T(8,128)S(1)} collective-permute-done((f32[4,8,6,128]{3,2,1,0:T(8,128)S(1)}, f32[4,8,6,128]{3,2,1,0:T(8,128)S(1)}, u32[]{:S(2)}, u32[]{:S(2)}) %collective-permute-start.3) | collective-permute-done | bytes 98336 | tf_op jit(solution)/shard_map/ppermute | solution.py:26
  54.5 1.8 fusion.195
  56.2 1.9 collective-permute-start.4
  58.2 3.9 collective-permute-start.5
  62.2 0.9 collective-permute-done.4
  63.1 6.2 %collective-permute-done.5 = f32[4,8,6,128]{3,2,1,0:T(8,128)S(1)} collective-permute-done((f32[4,8,6,128]{3,2,1,0:T(8,128)S(1)}, f32[4,8,6,128]{3,2,1,0:T(8,128)S(1)}, u32[]{:S(2)}, u32[]{:S(2)}) %collective-permute-start.5) | collective-permute-done | bytes 98336 | tf_op jit(solution)/shard_map/ppermute | solution.py:26
  69.3 1.6 fusion.134
  70.9 1.9 collective-permute-start.6
  72.9 3.9 collective-permute-start.7
  76.9 0.9 collective-permute-done.6
  77.8 6.8 %collective-permute-done.7 = f32[4,8,6,128]{3,2,1,0:T(8,128)S(1)} collective-permute-done((f32[4,8,6,128]{3,2,1,0:T(8,128)S(1)}, f32[4,8,6,128]{3,2,1,0:T(8,128)S(1)}, u32[]{:S(2)}, u32[]{:S(2)}) %collective-permute-start.7) | collective-permute-done | bytes 98336 | tf_op jit(solution)/shard_map/ppermute | solution.py:26
  85.5 1.9 collective-permute-start.8
  87.4 3.9 collective-permute-start.9
  91.4 0.9 collective-permute-done.8
  92.3 6.1 %collective-permute-done.9 = f32[4,8,6,128]{3,2,1,0:T(8,128)S(1)} collective-permute-done((f32[4,8,6,128]{3,2,1,0:T(8,128)S(1)}, f32[4,8,6,128]{3,2,1,0:T(8,128)S(1)}, u32[]{:S(2)}, u32[]{:S(2)}) %collective-permute-start.9) | collective-permute-done | bytes 98336 | tf_op jit(solution)/shard_map/ppermute | solution.py:26
  99.4 1.1 stack.11
  100.4 196.1 %all_to_all.5 = f32[32,2,4,8,8,128]{5,4,3,2,1,0:T(8,128)S(1)} all-to-all(f32[32,2,4,8,8,128]{5,4,3,2,1,0:T(8,128)S(1)} %stack.11), channel_id=1, replica_groups=mesh['band'=32,'dom'=16] {'band'}, dimensions={0} | all-to-all | bytes 16777216 | tf_op jit(solution)/shard_map/all_to_all | solution.py:79
  296.5 4.1 copy.7
  300.6 9.4 %reshape_reshape.3 = f32[256,8192]{1,0:T(8,128)} reshape(f32[2,32,4,8,8,128]{5,4,3,2,1,0:T(8,128)} %copy.7) | data formatting | bytes 16777216 | tf_op jit(solution)/shard_map/reshape;reshape | solution.py:81
  310.0 11.7 %fusion = f32[256,128]{1,0:T(8,128)S(1)} fusion(f32[256,8192]{1,0:T(8,128)} %reshape_reshape.3, f32[16,8,64,128]{3,2,1,0:T(8,128)} %bitcast.21), kind=kOutput, calls=%fused_computation | convolution fusion | flops 3221225472 | bytes 12713984 | tf_op jit(solution)/shard_map/dot_general | solution.py:82
  322.5 161.3 %all-reduce.7.cloned.1.call-done = f32[128,2,128]{2,0,1:T(8,128)} async-done(((f32[128,2,128]{2,0,1:T(8,128)}), f32[128,2,128]{2,0,1:T(8,128)}) %all-reduce.7.cloned.1.call-update) | async-done | bytes 131088 | tf_op jit(solution)/shard_map/psum | solution.py:90
  483.8 1.5 slice_bitcast_fusion
  (19 shorter events, 4.6 us)
Async XLA Ops:
  7.2 77.4 %copy-start = (f32[8,8,128]{2,1,0:T(8,128)S(1)}, f32[8,8,128]{2,1,0:T(8,128)}, u32[]{:S(2)}) copy-start(f32[8,8,128]{2,1,0:T(8,128)} %param.5) | copy-start | bytes 98308
  7.2 476.6 %all-reduce.7.cloned.1.call-start = ((), (), s32[]{:S(2)}) async-start(), calls=%async_computation.1 | async-start | bytes 262144 | tf_op jit(solution)/shard_map/psum | solution.py:90
  8.2 18.7 %collective-permute-start = (f32[4,8,6,128]{3,2,1,0:T(8,128)S(1)}, f32[4,8,6,128]{3,2,1,0:T(8,128)S(1)}, u32[]{:S(2)}, u32[]{:S(2)}) collective-permute-start(f32[4,8,6,128]{3,2,1,0:T(8,128)S(1)} %get-tuple-element.22), channel_id=1, source_target_pairs={{1,0},{2,1},{3,2},{4,3},{5,4},{6,5},{7,6},{8,7},{9,8},{10,9},{11,1... | collective-permute-start | bytes 294920 | tf_op jit(solution)/shard_map/ppermute | solution.py:29
  21.4 13.1 %collective-permute-start.1 = (f32[4,8,6,128]{3,2,1,0:T(8,128)S(1)}, f32[4,8,6,128]{3,2,1,0:T(8,128)S(1)}, u32[]{:S(2)}, u32[]{:S(2)}) collective-permute-start(f32[4,8,6,128]{3,2,1,0:T(8,128)S(1)} %get-tuple-element.23), channel_id=1, source_target_pairs={{0,1},{1,2},{2,3},{3,4},{4,5},{5,6},{6,7},{7,8},{8,9},{9,10},{10,1... | collective-permute-start | bytes 294920 | tf_op jit(solution)/shard_map/ppermute | solution.py:26
  39.7 7.8 %collective-permute-start.2 = (f32[4,8,6,128]{3,2,1,0:T(8,128)S(1)}, f32[4,8,6,128]{3,2,1,0:T(8,128)S(1)}, u32[]{:S(2)}, u32[]{:S(2)}) collective-permute-start(f32[4,8,6,128]{3,2,1,0:T(8,128)S(1)} %get-tuple-element.18), channel_id=1, source_target_pairs={{1,0},{2,1},{3,2},{4,3},{5,4},{6,5},{7,6},{8,7},{9,8},{10,9},{11,1... | collective-permute-start | bytes 294920 | tf_op jit(solution)/shard_map/ppermute | solution.py:29
  41.6 12.8 %collective-permute-start.3 = (f32[4,8,6,128]{3,2,1,0:T(8,128)S(1)}, f32[4,8,6,128]{3,2,1,0:T(8,128)S(1)}, u32[]{:S(2)}, u32[]{:S(2)}) collective-permute-start(f32[4,8,6,128]{3,2,1,0:T(8,128)S(1)} %get-tuple-element.19), channel_id=1, source_target_pairs={{0,1},{1,2},{2,3},{3,4},{4,5},{5,6},{6,7},{7,8},{8,9},{9,10},{10,1... | collective-permute-start | bytes 294920 | tf_op jit(solution)/shard_map/ppermute | solution.py:26
  56.2 6.9 %collective-permute-start.4 = (f32[4,8,6,128]{3,2,1,0:T(8,128)S(1)}, f32[4,8,6,128]{3,2,1,0:T(8,128)S(1)}, u32[]{:S(2)}, u32[]{:S(2)}) collective-permute-start(f32[4,8,6,128]{3,2,1,0:T(8,128)S(1)} %get-tuple-element.14), channel_id=1, source_target_pairs={{1,0},{2,1},{3,2},{4,3},{5,4},{6,5},{7,6},{8,7},{9,8},{10,9},{11,1... | collective-permute-start | bytes 294920 | tf_op jit(solution)/shard_map/ppermute | solution.py:29
  58.2 11.1 %collective-permute-start.5 = (f32[4,8,6,128]{3,2,1,0:T(8,128)S(1)}, f32[4,8,6,128]{3,2,1,0:T(8,128)S(1)}, u32[]{:S(2)}, u32[]{:S(2)}) collective-permute-start(f32[4,8,6,128]{3,2,1,0:T(8,128)S(1)} %get-tuple-element.15), channel_id=1, source_target_pairs={{0,1},{1,2},{2,3},{3,4},{4,5},{5,6},{6,7},{7,8},{8,9},{9,10},{10,1... | collective-permute-start | bytes 294920 | tf_op jit(solution)/shard_map/ppermute | solution.py:26
  70.9 6.9 %collective-permute-start.6 = (f32[4,8,6,128]{3,2,1,0:T(8,128)S(1)}, f32[4,8,6,128]{3,2,1,0:T(8,128)S(1)}, u32[]{:S(2)}, u32[]{:S(2)}) collective-permute-start(f32[4,8,6,128]{3,2,1,0:T(8,128)S(1)} %get-tuple-element.10), channel_id=1, source_target_pairs={{1,0},{2,1},{3,2},{4,3},{5,4},{6,5},{7,6},{8,7},{9,8},{10,9},{11,1... | collective-permute-start | bytes 294920 | tf_op jit(solution)/shard_map/ppermute | solution.py:29
  72.9 11.7 %collective-permute-start.7 = (f32[4,8,6,128]{3,2,1,0:T(8,128)S(1)}, f32[4,8,6,128]{3,2,1,0:T(8,128)S(1)}, u32[]{:S(2)}, u32[]{:S(2)}) collective-permute-start(f32[4,8,6,128]{3,2,1,0:T(8,128)S(1)} %get-tuple-element.11), channel_id=1, source_target_pairs={{0,1},{1,2},{2,3},{3,4},{4,5},{5,6},{6,7},{7,8},{8,9},{9,10},{10,1... | collective-permute-start | bytes 294920 | tf_op jit(solution)/shard_map/ppermute | solution.py:26
  85.5 6.9 %collective-permute-start.8 = (f32[4,8,6,128]{3,2,1,0:T(8,128)S(1)}, f32[4,8,6,128]{3,2,1,0:T(8,128)S(1)}, u32[]{:S(2)}, u32[]{:S(2)}) collective-permute-start(f32[4,8,6,128]{3,2,1,0:T(8,128)S(1)} %get-tuple-element.6), channel_id=1, source_target_pairs={{1,0},{2,1},{3,2},{4,3},{5,4},{6,5},{7,6},{8,7},{9,8},{10,9},{11,1... | collective-permute-start | bytes 294920 | tf_op jit(solution)/shard_map/ppermute | solution.py:29
  87.4 11.1 %collective-permute-start.9 = (f32[4,8,6,128]{3,2,1,0:T(8,128)S(1)}, f32[4,8,6,128]{3,2,1,0:T(8,128)S(1)}, u32[]{:S(2)}, u32[]{:S(2)}) collective-permute-start(f32[4,8,6,128]{3,2,1,0:T(8,128)S(1)} %get-tuple-element.7), channel_id=1, source_target_pairs={{0,1},{1,2},{2,3},{3,4},{4,5},{5,6},{6,7},{7,8},{8,9},{9,10},{10,1... | collective-permute-start | bytes 294920 | tf_op jit(solution)/shard_map/ppermute | solution.py:26
Sparse Core Ops, SparseCore 0:
  322.6 161.1 all-reduce.6
